TPU v7x, 32 devices: a whole 2x2x4 slice. The times are simulated.
32 devices in a mesh: groups: 2 (over y), tile: 4 (over z), image: 4 (over x, core).
Axes of the slice: x: 2, y: 2, z: 4, core: 2. Of those that a mesh axis runs over, the one named last changes fastest.
Arguments:
- images: bfloat16 [8, 16, 64, 256], P(('groups', 'image'), 'tile'), parts along dimension 0, may hold values from -12 to 12
- cotangent: bfloat16 [8, 16, 64, 256], P(('groups', 'image'), 'tile'), parts along dimension 0, may hold values from -12 to 12
- timesteps: int32 [8], P(('groups', 'image')), parts along dimension 0, may hold values from 0 to 999
- class_ids: int32 [8], P(('groups', 'image')), parts along dimension 0, may hold values from 0 to 999
- norm_gain: float32 [256], replicated, may hold values from 0.25 to 1.75
- norm_bias: float32 [256], replicated, may hold values from -3 to 3
- conv_first: bfloat16 [3, 3, 256, 256], replicated, may hold values from -0.125 to 0.125
- conv_second: bfloat16 [3, 3, 256, 256], replicated, may hold values from -0.125 to 0.125
- time_weight: bfloat16 [256, 1024], P(None, 'tile'), may hold values from -0.375 to 0.375
- time_bias: float32 [1024], P('tile'), may hold values from -3 to 3
- class_table: bfloat16 [1000, 1024], P(None, 'tile'), may hold values from -5 to 5
- adaptive_weight: bfloat16 [1024, 512], P('tile'), may hold values from -0.1875 to 0.1875
- adaptive_bias: float32 [512], replicated, may hold values from -2 to 2
Outputs:
- branch: bfloat16 [8, 16, 64, 256], P(('groups', 'image'), 'tile'), parts along dimension 0
- input_grad: bfloat16 [8, 16, 64, 256], P(('groups', 'image'), 'tile'), parts along dimension 0
- grad_adaptive_weight: float32 [2048, 512], P(('groups', 'tile')), parts along dimension 0
- grad_adaptive_bias: float32 [1024], P('groups'), parts along dimension 0
There are 2 independent parts, one for each index of `groups`. A program takes and returns all parts, laid end to end along the dimension named above; an argument that names none is the same for every part. Nothing has to cross between parts.
All inputs are finite; a program needn't handle non-finite values.
Results may differ from a plain program's by a relative error of at most 0.013.
Values may be sent and summed in bfloat16 or wider, within the bound.
A program may use at most 64 MiB of HBM per device.

v0:
```python
import math
import jax
import jax.numpy as jnp
from jax import lax
from jax.sharding import PartitionSpec as P

GN_GROUPS = 32
EPSILON = 1e-05


def with_halo(block, sides, width):
    for axis, dim in sides:
        count = lax.axis_size(axis)
        forward = [(i, i + 1) for i in range(count - 1)]
        backward = [(target, source) for source, target in forward]
        low = lax.ppermute(
            lax.slice_in_dim(block, block.shape[dim] - width, None, axis=dim), axis, forward
        )
        high = lax.ppermute(lax.slice_in_dim(block, 0, width, axis=dim), axis, backward)
        block = jnp.concatenate([low, block, high], axis=dim)
    return block


def silu_grad(pre_values):
    sigma = jax.nn.sigmoid(pre_values)
    return sigma * (1.0 + pre_values * (1.0 - sigma))


def conv_rows(padded, kernel):
    row_count = padded.shape[1] - 2
    col_count = padded.shape[2]
    channels = padded.shape[3]
    padded_cols = jnp.pad(padded, ((0, 0), (0, 0), (1, 1), (0, 0)))
    widened = jnp.concatenate(
        [padded_cols[:, :, offset : offset + col_count] for offset in range(3)], axis=3
    )
    summed = None
    for offset in range(3):
        row_block = widened[:, offset : offset + row_count].reshape(-1, 3 * channels)
        product = jnp.dot(
            row_block, kernel[offset].reshape(3 * channels, -1), preferred_element_type=jnp.float32
        )
        summed = product if summed is None else summed + product
    return summed.reshape(padded.shape[0], row_count, col_count, -1)


def group_total(values):
    return values.reshape(values.shape[0], GN_GROUPS, -1).sum(axis=2)


def spread_groups(values, channels):
    return jnp.repeat(values, channels // GN_GROUPS, axis=1)[:, None, None, :]


def cell_total(values):
    return (
        values.shape[1] * values.shape[2] * lax.axis_size("tile") * (values.shape[3] // GN_GROUPS)
    )


def moments(values):
    channels = values.shape[3]
    cell_count = cell_total(values)
    first_sum = group_total(jnp.sum(values, axis=(1, 2)))
    square_sum = group_total(jnp.sum(values * values, axis=(1, 2)))
    first_sum, square_sum = lax.psum((first_sum, square_sum), "tile")
    centre = first_sum / cell_count
    spread = square_sum / cell_count - centre * centre
    centre = spread_groups(centre, channels)
    return (centre, spread_groups(lax.rsqrt(spread + EPSILON), channels))


def with_rims(active):
    return with_halo(active, (("tile", 1),), 1)


def first_rims(active, cotangent):
    padded_first = with_rims(active)
    padded_grad = with_halo(cotangent, (("tile", 1),), 1)
    return (padded_first, padded_grad)


def norm_back_first(grad_norm, normed, inverse):
    channels = grad_norm.shape[3]
    cell_count = cell_total(grad_norm)
    plain_sum = group_total(jnp.sum(grad_norm, axis=(1, 2)))
    paired_sum = group_total(jnp.sum(grad_norm * normed, axis=(1, 2)))
    plain_sum, paired_sum = lax.psum((plain_sum, paired_sum), "tile")
    return inverse * (
        grad_norm
        - spread_groups(plain_sum / cell_count, channels)
        - normed * spread_groups(paired_sum / cell_count, channels)
    )


def body(
    images,
    cotangent,
    timesteps,
    class_ids,
    norm_gain,
    norm_bias,
    conv_first,
    conv_second,
    time_weight,
    time_bias,
    class_table,
    adaptive_weight,
    adaptive_bias,
):
    channels = images.shape[3]
    half_freq = time_weight.shape[0] // 2
    frequencies = jnp.exp(-math.log(10000.0) * jnp.arange(half_freq, dtype=jnp.float32) / half_freq)
    angles = timesteps.astype(jnp.float32)[:, None] * frequencies[None]
    sinusoid = jnp.concatenate([jnp.cos(angles), jnp.sin(angles)], axis=1)
    hidden = (
        jnp.dot(sinusoid, time_weight.astype(jnp.float32), precision=lax.Precision.HIGHEST)
        + time_bias
    )
    onehot = (class_ids[:, None] == jnp.arange(class_table.shape[0], dtype=jnp.int32)[None]).astype(
        jnp.float32
    )
    embedding = jax.nn.silu(hidden) + jnp.dot(
        onehot, class_table.astype(jnp.float32), precision=lax.Precision.HIGHEST
    )
    activated = jax.nn.silu(embedding)
    partial_terms = jnp.dot(
        activated, adaptive_weight.astype(jnp.float32), precision=lax.Precision.HIGHEST
    )
    modulation = lax.psum(partial_terms, "tile") + adaptive_bias
    factor_row = 1.0 + modulation[:, :channels]
    factor = factor_row[:, None, None, :]
    shift_term = modulation[:, channels:][:, None, None, :]
    input_float = images.astype(jnp.float32)
    centre_first, inverse_first = moments(input_float)
    normed_first = (input_float - centre_first) * inverse_first
    pre_first = normed_first * norm_gain + norm_bias
    active_first = jax.nn.silu(pre_first).astype(jnp.bfloat16)
    padded_first, padded_grad = first_rims(active_first, cotangent)
    hidden_first = conv_rows(padded_first, conv_first).astype(jnp.bfloat16)
    hidden_float = hidden_first.astype(jnp.float32)
    centre_second, inverse_second = moments(hidden_float)
    normed_second = (hidden_float - centre_second) * inverse_second
    pre_second = normed_second * factor + shift_term
    active_second = jax.nn.silu(pre_second).astype(jnp.bfloat16)
    padded_second = with_rims(active_second)
    branch = conv_rows(padded_second, conv_second).astype(jnp.bfloat16)
    flipped_second = jnp.flip(conv_second, (0, 1)).transpose(0, 1, 3, 2)
    grad_active = conv_rows(padded_grad, flipped_second)
    grad_pre = grad_active * silu_grad(pre_second)
    scale_sum = jnp.sum(grad_pre * normed_second, axis=(1, 2))
    shift_sum = jnp.sum(grad_pre, axis=(1, 2))
    scale_sum, shift_sum = lax.psum((scale_sum, shift_sum), "tile")
    cell_count = cell_total(grad_pre)
    plain_mean = group_total(shift_sum * factor_row) / cell_count
    paired_mean = group_total(scale_sum * factor_row) / cell_count
    grad_norm = grad_pre * factor
    grad_hidden = (
        inverse_second
        * (
            grad_norm
            - spread_groups(plain_mean, channels)
            - normed_second * spread_groups(paired_mean, channels)
        )
    ).astype(jnp.bfloat16)
    flipped_first = jnp.flip(conv_first, (0, 1)).transpose(0, 1, 3, 2)
    padded_hidden = with_halo(grad_hidden, (("tile", 1),), 1)
    grad_active_first = conv_rows(padded_hidden, flipped_first)
    grad_first = grad_active_first * silu_grad(pre_first) * norm_gain
    input_grad = norm_back_first(grad_first, normed_first, inverse_first).astype(jnp.bfloat16)
    pairs = jnp.concatenate([scale_sum, shift_sum], axis=1)
    local_weight = jnp.dot(activated.T, pairs, precision=lax.Precision.HIGHEST)
    local_bias = jnp.sum(pairs, axis=0)
    grad_weight, grad_bias = (
        lax.psum(local_weight.astype(jnp.bfloat16), "image").astype(jnp.float32),
        lax.psum(local_bias.astype(jnp.bfloat16), "image").astype(jnp.float32),
    )
    return (branch, input_grad, grad_weight, grad_bias)


def solution(mesh):
    return jax.shard_map(
        body,
        mesh=mesh,
        in_specs=(
            P(("groups", "image"), "tile", None, None),
            P(("groups", "image"), "tile", None, None),
            P(("groups", "image")),
            P(("groups", "image")),
            P(),
            P(),
            P(),
            P(),
            P(None, "tile"),
            P("tile"),
            P(None, "tile"),
            P("tile", None),
            P(),
        ),
        out_specs=(
            P(("groups", "image"), "tile", None, None),
            P(("groups", "image"), "tile", None, None),
            P(("groups", "tile"), None),
            P("groups"),
        ),
        check_vma=False,
    )
```

profile of v0, /device:TPU:0, one launch (start us, length us, event | category | flops | bytes accessed | tf_op | source)
XLA Modules:
  0.0 125.2 jit_solution(5303490498117019014)
XLA Ops:
  7.2 1.0 convert_reduce_fusion
  8.6 13.5 %all-reduce.7 = (f32[1,32]{1,0:T(1,128)S(1)}, f32[1,32]{1,0:T(1,128)S(1)}) all-reduce(f32[1,32]{1,0:T(1,128)S(1)} %bitcast.139, f32[1,32]{1,0:T(1,128)S(1)} %bitcast.141), channel_id=1, replica_groups=mesh['groups'=2,'tile'=4,'image'=4] {'tile'}, use_global_device_ids=true, to_apply=%region_5.6 | all-reduce | flops 64 | bytes 512 | tf_op jit(solution)/shard_map/psum | solution.py:66
  22.5 1.0 fusion.15
  24.1 1.3 %collective-permute-start.1 = (bf16[1,1,64,256]{3,2,1,0:T(8,128)(2,1)}, bf16[1,1,64,256]{3,2,1,0:T(8,128)(2,1)S(1)}, u32[]{:S(2)}, u32[]{:S(2)}) collective-permute-start(bf16[1,1,64,256]{3,2,1,0:T(8,128)(2,1)} %get-tuple-element.65), channel_id=1, source_target_pairs={{4,0},{8,4},{12,8},{5,1},{9,5},{13,9},{6,2},{10,6},{14,10},{7,3},{... | collective-permute-start | bytes 98312 | tf_op jit(solution)/shard_map/ppermute | solution.py:19
  25.4 4.5 %collective-permute-start = (bf16[1,1,64,256]{3,2,1,0:T(8,128)(2,1)}, bf16[1,1,64,256]{3,2,1,0:T(8,128)(2,1)S(1)}, u32[]{:S(2)}, u32[]{:S(2)}) collective-permute-start(bf16[1,1,64,256]{3,2,1,0:T(8,128)(2,1)} %get-tuple-element.64), channel_id=1, source_target_pairs={{0,4},{4,8},{8,12},{1,5},{5,9},{9,13},{2,6},{6,10},{10,14},{3,7},{... | collective-permute-start | bytes 98312 | tf_op jit(solution)/shard_map/ppermute | solution.py:16
  30.0 1.4 %fusion.53 = (bf16[1,1,64,256]{3,2,1,0:T(8,128)(2,1)}, bf16[1,1,64,256]{3,2,1,0:T(8,128)(2,1)}) fusion(bf16[1,4,64,256]{3,2,1,0:T(8,128)(2,1)} %param.14), kind=kLoop, calls=%fused_computation.107 | loop fusion | bytes 131072 | tf_op jit(solution)/shard_map/slice | solution.py:19
  31.4 1.9 %collective-permute-start.4 = (bf16[1,1,64,256]{3,2,1,0:T(8,128)(2,1)}, bf16[1,1,64,256]{3,2,1,0:T(8,128)(2,1)S(1)}, u32[]{:S(2)}, u32[]{:S(2)}) collective-permute-start(bf16[1,1,64,256]{3,2,1,0:T(8,128)(2,1)} %get-tuple-element.61), channel_id=1, source_target_pairs={{0,4},{4,8},{8,12},{1,5},{5,9},{9,13},{2,6},{6,10},{10,14},{3,7},{... | collective-permute-start | bytes 98312 | tf_op jit(solution)/shard_map/ppermute | solution.py:16
  33.3 1.4 %collective-permute-start.5 = (bf16[1,1,64,256]{3,2,1,0:T(8,128)(2,1)}, bf16[1,1,64,256]{3,2,1,0:T(8,128)(2,1)S(1)}, u32[]{:S(2)}, u32[]{:S(2)}) collective-permute-start(bf16[1,1,64,256]{3,2,1,0:T(8,128)(2,1)} %get-tuple-element.60), channel_id=1, source_target_pairs={{4,0},{8,4},{12,8},{5,1},{9,5},{13,9},{6,2},{10,6},{14,10},{7,3},{... | collective-permute-start | bytes 98312 | tf_op jit(solution)/shard_map/ppermute | solution.py:19
  34.7 2.4 %copy.17 = bf16[3,3,256,256]{2,3,1,0:T(8,128)(2,1)} copy(bf16[3,3,256,256]{3,2,1,0:T(8,128)(2,1)} %param.20) | data formatting | bytes 2359296 | tf_op args[7]
  37.1 1.0 fusion.43
  38.7 1.0 fusion.44
  39.7 1.6 %copy.18 = bf16[3,3,256,256]{2,3,1,0:T(8,128)(2,1)} copy(bf16[3,3,256,256]{3,2,1,0:T(8,128)(2,1)S(1)} %copy-done.2) | data formatting | bytes 2359296 | tf_op args[6]
  42.8 1.0 fusion.42
  48.7 11.0 %all-reduce.6 = (f32[1,512]{1,0:T(1,128)S(1)}, f32[1,32]{1,0:T(1,128)S(1)}, f32[1,32]{1,0:T(1,128)S(1)}) all-reduce(f32[1,512]{1,0:T(1,128)S(1)} %fusion.58, f32[1,32]{1,0:T(1,128)S(1)} %bitcast.134, f32[1,32]{1,0:T(1,128)S(1)} %bitcast.135), channel_id=1, replica_groups=mesh['groups'=2,'tile'=4,'image'=4] {'tile'}, use_global_device_ids=true, to_apply=%region_12.13 | all-reduce | flops 576 | bytes 4608 | tf_op jit(solution)/shard_map/psum | solution.py:130
  62.6 8.5 %all-reduce.5 = (f32[1,256]{1,0:T(1,128)S(1)}, f32[1,256]{1,0:T(1,128)S(1)}) all-reduce(f32[1,256]{1,0:T(1,128)S(1)} %bitcast.136, f32[1,256]{1,0:T(1,128)S(1)} %bitcast.137), channel_id=1, replica_groups=mesh['groups'=2,'tile'=4,'image'=4] {'tile'}, use_global_device_ids=true, to_apply=%region_14.15 | all-reduce | flops 512 | bytes 4096 | tf_op jit(solution)/shard_map/psum | solution.py:153
  72.1 1.3 %collective-permute-start.3 = (bf16[1,1,64,256]{3,2,1,0:T(8,128)(2,1)S(1)}, bf16[1,1,64,256]{3,2,1,0:T(8,128)(2,1)S(1)}, u32[]{:S(2)}, u32[]{:S(2)}) collective-permute-start(bf16[1,1,64,256]{3,2,1,0:T(8,128)(2,1)S(1)} %get-tuple-element.63), channel_id=1, source_target_pairs={{4,0},{8,4},{12,8},{5,1},{9,5},{13,9},{6,2},{10,6},{14,10},{7,3},{... | collective-permute-start | bytes 98312 | tf_op jit(solution)/shard_map/ppermute | solution.py:19
  73.4 4.5 %collective-permute-start.2 = (bf16[1,1,64,256]{3,2,1,0:T(8,128)(2,1)S(1)}, bf16[1,1,64,256]{3,2,1,0:T(8,128)(2,1)S(1)}, u32[]{:S(2)}, u32[]{:S(2)}) collective-permute-start(bf16[1,1,64,256]{3,2,1,0:T(8,128)(2,1)S(1)} %get-tuple-element.62), channel_id=1, source_target_pairs={{0,4},{4,8},{8,12},{1,5},{5,9},{9,13},{2,6},{6,10},{10,14},{3,7},{... | collective-permute-start | bytes 98312 | tf_op jit(solution)/shard_map/ppermute | solution.py:16
  78.8 1.3 %collective-permute-start.7 = (bf16[1,1,64,256]{3,2,1,0:T(8,128)(2,1)S(1)}, bf16[1,1,64,256]{3,2,1,0:T(8,128)(2,1)S(1)}, u32[]{:S(2)}, u32[]{:S(2)}) collective-permute-start(bf16[1,1,64,256]{3,2,1,0:T(8,128)(2,1)S(1)} %get-tuple-element.59), channel_id=1, source_target_pairs={{4,0},{8,4},{12,8},{5,1},{9,5},{13,9},{6,2},{10,6},{14,10},{7,3},{... | collective-permute-start | bytes 98312 | tf_op jit(solution)/shard_map/ppermute | solution.py:19
  80.1 4.5 %collective-permute-start.6 = (bf16[1,1,64,256]{3,2,1,0:T(8,128)(2,1)S(1)}, bf16[1,1,64,256]{3,2,1,0:T(8,128)(2,1)S(1)}, u32[]{:S(2)}, u32[]{:S(2)}) collective-permute-start(bf16[1,1,64,256]{3,2,1,0:T(8,128)(2,1)S(1)} %get-tuple-element.58), channel_id=1, source_target_pairs={{0,4},{4,8},{8,12},{1,5},{5,9},{9,13},{2,6},{6,10},{10,14},{3,7},{... | collective-permute-start | bytes 98312 | tf_op jit(solution)/shard_map/ppermute | solution.py:16
  84.6 5.7 %psum.87 = bf16[512]{0:T(512)(128)(2,1)S(1)} all-reduce(bf16[512]{0:T(512)(128)(2,1)S(1)} %convert_element_type.135), channel_id=1, replica_groups=mesh['groups'=2,'tile'=4,'image'=4] {'image'}, use_global_device_ids=true, to_apply=%region_26.27 | all-reduce | flops 512 | bytes 2048 | tf_op jit(solution)/shard_map/psum | solution.py:176
  94.0 10.2 %all-reduce.4 = (f32[1,32]{1,0:T(1,128)S(1)}, f32[1,32]{1,0:T(1,128)S(1)}) all-reduce(f32[1,32]{1,0:T(1,128)S(1)} %bitcast.138, f32[1,32]{1,0:T(1,128)S(1)} %bitcast.140), channel_id=1, replica_groups=mesh['groups'=2,'tile'=4,'image'=4] {'tile'}, use_global_device_ids=true, to_apply=%region_24.25 | all-reduce | flops 64 | bytes 512 | tf_op jit(solution)/shard_map/psum | solution.py:88
  105.2 0.9 fusion.2
  106.9 9.7 %all-reduce.10.cloned.1.call-done = bf16[256,512]{1,0:T(8,128)(2,1)} async-done(((bf16[256,512]{1,0:T(8,128)(2,1)}), bf16[256,512]{1,0:T(8,128)(2,1)}) %all-reduce.10.cloned.1.call-update) | async-done | bytes 262160 | tf_op jit(solution)/shard_map/psum | solution.py:175
  116.6 1.8 %convert_element_type.134 = f32[256,512]{1,0:T(8,128)} convert(bf16[256,512]{1,0:T(8,128)(2,1)} %all-reduce.10.cloned.1.call-done) | non-fusion elementwise | flops 131072 | bytes 786432 | tf_op jit(solution)/shard_map/convert_element_type | solution.py:175
  (142 shorter events, 16.7 us)
Async XLA Ops:
  7.2 37.4 %copy-start = (bf16[1000,256]{1,0:T(8,128)(2,1)S(1)}, bf16[1000,256]{1,0:T(8,128)(2,1)}, u32[]{:S(2)}) copy-start(bf16[1000,256]{1,0:T(8,128)(2,1)} %param.23) | copy-start | bytes 1536004
  7.2 109.4 %all-reduce.10.cloned.1.call-start = ((), (), s32[]{:S(2)}) async-start(), calls=%async_computation | async-start | bytes 524288 | tf_op jit(solution)/shard_map/psum | solution.py:175
  24.1 21.6 %collective-permute-start.1 = (bf16[1,1,64,256]{3,2,1,0:T(8,128)(2,1)}, bf16[1,1,64,256]{3,2,1,0:T(8,128)(2,1)S(1)}, u32[]{:S(2)}, u32[]{:S(2)}) collective-permute-start(bf16[1,1,64,256]{3,2,1,0:T(8,128)(2,1)} %get-tuple-element.65), channel_id=1, source_target_pairs={{4,0},{8,4},{12,8},{5,1},{9,5},{13,9},{6,2},{10,6},{14,10},{7,3},{... | collective-permute-start | bytes 98312 | tf_op jit(solution)/shard_map/ppermute | solution.py:19
  25.4 20.4 %collective-permute-start = (bf16[1,1,64,256]{3,2,1,0:T(8,128)(2,1)}, bf16[1,1,64,256]{3,2,1,0:T(8,128)(2,1)S(1)}, u32[]{:S(2)}, u32[]{:S(2)}) collective-permute-start(bf16[1,1,64,256]{3,2,1,0:T(8,128)(2,1)} %get-tuple-element.64), channel_id=1, source_target_pairs={{0,4},{4,8},{8,12},{1,5},{5,9},{9,13},{2,6},{6,10},{10,14},{3,7},{... | collective-permute-start | bytes 98312 | tf_op jit(solution)/shard_map/ppermute | solution.py:16
  31.4 28.4 %collective-permute-start.4 = (bf16[1,1,64,256]{3,2,1,0:T(8,128)(2,1)}, bf16[1,1,64,256]{3,2,1,0:T(8,128)(2,1)S(1)}, u32[]{:S(2)}, u32[]{:S(2)}) collective-permute-start(bf16[1,1,64,256]{3,2,1,0:T(8,128)(2,1)} %get-tuple-element.61), channel_id=1, source_target_pairs={{0,4},{4,8},{8,12},{1,5},{5,9},{9,13},{2,6},{6,10},{10,14},{3,7},{... | collective-permute-start | bytes 98312 | tf_op jit(solution)/shard_map/ppermute | solution.py:16
  33.3 3.8 %copy-start.1 = (bf16[3,3,256,256]{3,2,1,0:T(8,128)(2,1)S(1)}, bf16[3,3,256,256]{3,2,1,0:T(8,128)(2,1)}, u32[]{:S(2)}) copy-start(bf16[3,3,256,256]{3,2,1,0:T(8,128)(2,1)} %param.20) | copy-start | bytes 3538948
  33.3 26.8 %collective-permute-start.5 = (bf16[1,1,64,256]{3,2,1,0:T(8,128)(2,1)}, bf16[1,1,64,256]{3,2,1,0:T(8,128)(2,1)S(1)}, u32[]{:S(2)}, u32[]{:S(2)}) collective-permute-start(bf16[1,1,64,256]{3,2,1,0:T(8,128)(2,1)} %get-tuple-element.60), channel_id=1, source_target_pairs={{4,0},{8,4},{12,8},{5,1},{9,5},{13,9},{6,2},{10,6},{14,10},{7,3},{... | collective-permute-start | bytes 98312 | tf_op jit(solution)/shard_map/ppermute | solution.py:19
  37.1 1.6 %copy-start.2 = (bf16[3,3,256,256]{3,2,1,0:T(8,128)(2,1)S(1)}, bf16[3,3,256,256]{3,2,1,0:T(8,128)(2,1)}, u32[]{:S(2)}) copy-start(bf16[3,3,256,256]{3,2,1,0:T(8,128)(2,1)} %param.19) | copy-start | bytes 3538948
  39.7 3.0 %copy-start.3 = (bf16[3,3,256,256]{2,3,1,0:T(8,128)(2,1)S(1)}, bf16[3,3,256,256]{2,3,1,0:T(8,128)(2,1)}, u32[]{:S(2)}) copy-start(bf16[3,3,256,256]{2,3,1,0:T(8,128)(2,1)} %copy.17) | copy-start | bytes 3538948
  42.8 1.6 %copy-start.4 = (bf16[3,3,256,256]{2,3,1,0:T(8,128)(2,1)S(1)}, bf16[3,3,256,256]{2,3,1,0:T(8,128)(2,1)}, u32[]{:S(2)}) copy-start(bf16[3,3,256,256]{2,3,1,0:T(8,128)(2,1)} %copy.18) | copy-start | bytes 3538948
  44.4 1.0 copy-start.20
  44.5 1.1 copy-start.15
  46.0 1.0 copy-start.12
  46.0 1.3 %copy-start.11 = (bf16[1,3,256,256]{3,2,1,0:T(8,128)(2,1)S(1)}, bf16[1,3,256,256]{3,2,1,0:T(8,128)(2,1)}, u32[]{:S(2)}) copy-start(bf16[1,3,256,256]{3,2,1,0:T(8,128)(2,1)} %get-tuple-element.34) | copy-start | bytes 1179652
  47.0 1.0 copy-start.10
  47.3 12.5 %copy-start.19 = (f32[512]{0:T(512)S(1)}, f32[512]{0:T(512)}, u32[]{:S(2)}) copy-start(f32[512]{0:T(512)} %param.25) | copy-start | bytes 6148
  47.3 12.5 %copy-start.14 = (bf16[1,4,64,256]{3,2,1,0:T(8,128)(2,1)S(1)}, bf16[1,4,64,256]{3,2,1,0:T(8,128)(2,1)}, u32[]{:S(2)}) copy-start(bf16[1,4,64,256]{3,2,1,0:T(8,128)(2,1)} %param.14) | copy-start | bytes 393220
  72.1 18.8 %collective-permute-start.3 = (bf16[1,1,64,256]{3,2,1,0:T(8,128)(2,1)S(1)}, bf16[1,1,64,256]{3,2,1,0:T(8,128)(2,1)S(1)}, u32[]{:S(2)}, u32[]{:S(2)}) collective-permute-start(bf16[1,1,64,256]{3,2,1,0:T(8,128)(2,1)S(1)} %get-tuple-element.63), channel_id=1, source_target_pairs={{4,0},{8,4},{12,8},{5,1},{9,5},{13,9},{6,2},{10,6},{14,10},{7,3},{... | collective-permute-start | bytes 98312 | tf_op jit(solution)/shard_map/ppermute | solution.py:19
  73.4 17.5 %collective-permute-start.2 = (bf16[1,1,64,256]{3,2,1,0:T(8,128)(2,1)S(1)}, bf16[1,1,64,256]{3,2,1,0:T(8,128)(2,1)S(1)}, u32[]{:S(2)}, u32[]{:S(2)}) collective-permute-start(bf16[1,1,64,256]{3,2,1,0:T(8,128)(2,1)S(1)} %get-tuple-element.62), channel_id=1, source_target_pairs={{0,4},{4,8},{8,12},{1,5},{5,9},{9,13},{2,6},{6,10},{10,14},{3,7},{... | collective-permute-start | bytes 98312 | tf_op jit(solution)/shard_map/ppermute | solution.py:16
  78.8 13.2 %collective-permute-start.7 = (bf16[1,1,64,256]{3,2,1,0:T(8,128)(2,1)S(1)}, bf16[1,1,64,256]{3,2,1,0:T(8,128)(2,1)S(1)}, u32[]{:S(2)}, u32[]{:S(2)}) collective-permute-start(bf16[1,1,64,256]{3,2,1,0:T(8,128)(2,1)S(1)} %get-tuple-element.59), channel_id=1, source_target_pairs={{4,0},{8,4},{12,8},{5,1},{9,5},{13,9},{6,2},{10,6},{14,10},{7,3},{... | collective-permute-start | bytes 98312 | tf_op jit(solution)/shard_map/ppermute | solution.py:19
  80.1 11.9 %collective-permute-start.6 = (bf16[1,1,64,256]{3,2,1,0:T(8,128)(2,1)S(1)}, bf16[1,1,64,256]{3,2,1,0:T(8,128)(2,1)S(1)}, u32[]{:S(2)}, u32[]{:S(2)}) collective-permute-start(bf16[1,1,64,256]{3,2,1,0:T(8,128)(2,1)S(1)} %get-tuple-element.58), channel_id=1, source_target_pairs={{0,4},{4,8},{8,12},{1,5},{5,9},{9,13},{2,6},{6,10},{10,14},{3,7},{... | collective-permute-start | bytes 98312 | tf_op jit(solution)/shard_map/ppermute | solution.py:16
  92.8 11.8 %copy-start.7 = (bf16[1,3,256,256]{3,2,1,0:T(8,128)(2,1)S(1)}, bf16[1,3,256,256]{3,2,1,0:T(8,128)(2,1)}, u32[]{:S(2)}) copy-start(bf16[1,3,256,256]{3,2,1,0:T(8,128)(2,1)} %get-tuple-element.32) | copy-start | bytes 1179652
  92.8 11.8 %copy-start.9 = (bf16[1,4,64,768]{3,2,1,0:T(8,128)(2,1)S(1)}, bf16[1,4,64,768]{3,2,1,0:T(8,128)(2,1)}, u32[]{:S(2)}) copy-start(bf16[1,4,64,768]{3,2,1,0:T(8,128)(2,1)} %get-tuple-element.44) | copy-start | bytes 1179652
  93.4 11.5 %copy-start.6 = (bf16[1,3,256,256]{3,2,1,0:T(8,128)(2,1)S(1)}, bf16[1,3,256,256]{3,2,1,0:T(8,128)(2,1)}, u32[]{:S(2)}) copy-start(bf16[1,3,256,256]{3,2,1,0:T(8,128)(2,1)} %get-tuple-element.31) | copy-start | bytes 1179652
  (6 other events, 5.6 us)
Sparse Core Ops, SparseCore 0:
  84.8 31.7 all-reduce.9
where the time goes:
time: 126 us; the launch traced here: 125 us
  blocking collectives  48.9 us (39%)
  starting transfers between devices  20.9 us (17%)
  local copies, waits for them, and re-layouts  17.4 us (14%)
  between operations  16 us (13%)
  waiting for transfers between devices  9.77 us (8%)
  other arithmetic  7.85 us (6%)
  matrix products  4.46 us (4%)
    ppermute x4, starting transfers between devices, with_halo(): lax.ppermute(lax.slice_in_dim(block, block.shape[dim] - width, None, axis...  15.6 us
    psum x1, blocking collectives, moments(): first_sum, square_sum = lax.psum((first_sum, square_sum), 'tile')  13.5 us
    psum x1, blocking collectives, body(): modulation = lax.psum(partial_terms, 'tile') + adaptive_bias  11 us
    psum x1, blocking collectives, norm_back_first(): plain_sum, paired_sum = lax.psum((plain_sum, paired_sum), 'tile')  10.2 us
    psum x1, waiting for transfers between devices, body(): lax.psum(local_weight.astype(jnp.bfloat16), 'image').astype(jnp.float32)  9.73 us
    unnamed x46, local copies, waits for them, and re-layouts  8.78 us
    psum x1, blocking collectives, body(): scale_sum, shift_sum = lax.psum((scale_sum, shift_sum), 'tile')  8.47 us
    psum x1, blocking collectives, body(): lax.psum(local_bias.astype(jnp.bfloat16), 'image').astype(jnp.float32)  5.67 us
  transfers between devices with their start and end apart: 9, of which 1 were waited for; matrix products, arithmetic and copies ran while one was open for 14% of the time, Pallas kernels for 0%

commit v1 on v0

--- a/solution.py
+++ b/solution.py
@@ -127,7 +127,7 @@
     partial_terms = jnp.dot(
         activated, adaptive_weight.astype(jnp.float32), precision=lax.Precision.HIGHEST
     )
-    modulation = lax.psum(partial_terms, "tile") + adaptive_bias
+    modulation = jnp.sum(lax.all_gather(partial_terms, "tile"), axis=0) + adaptive_bias
     factor_row = 1.0 + modulation[:, :channels]
     factor = factor_row[:, None, None, :]
     shift_term = modulation[:, channels:][:, None, None, :]

time: 126 us -> 139 us (1.10)
  blocking collectives: 48.9 us -> 59.9 us
  matrix products: 4.46 us -> 6.33 us
    all_gather x0 -> x1, blocking collectives: none -> 11.9 us  [body(): lax.all_gather(partial_terms, 'tile')]
    psum x1 -> x0, blocking collectives: 11 us -> none  [body(): modulation = lax.psum(partial_terms, 'tile') + adaptive_bias]
    psum x1 -> x2, blocking collectives: 13.5 us -> 23.6 us  [moments(): first_sum, square_sum = lax.psum((first_sum, square_sum), 'tile')]
    unnamed x46 -> x42, local copies, waits for them, and re-layouts: 8.78 us -> 8.76 us
where the time goes in v1:
time: 139 us; the launch traced here: 138 us
  blocking collectives  59.9 us (43%)
  starting transfers between devices  20.9 us (15%)
  local copies, waits for them, and re-layouts  17.4 us (13%)
  between operations  15.9 us (11%)
  waiting for transfers between devices  9.77 us (7%)
  other arithmetic  7.87 us (6%)
  matrix products  6.33 us (5%)
    psum x2, blocking collectives, moments(): first_sum, square_sum = lax.psum((first_sum, square_sum), 'tile')  23.6 us
    ppermute x4, starting transfers between devices, with_halo(): lax.ppermute(lax.slice_in_dim(block, block.shape[dim] - width, None, axis...  15.6 us
    all_gather x1, blocking collectives, body(): lax.all_gather(partial_terms, 'tile')  11.9 us
    psum x1, blocking collectives, norm_back_first(): plain_sum, paired_sum = lax.psum((plain_sum, paired_sum), 'tile')  10.1 us
    psum x1, waiting for transfers between devices, body(): lax.psum(local_weight.astype(jnp.bfloat16), 'image').astype(jnp.float32)  9.73 us
    unnamed x42, local copies, waits for them, and re-layouts  8.76 us
    psum x1, blocking collectives, body(): scale_sum, shift_sum = lax.psum((scale_sum, shift_sum), 'tile')  8.66 us
    psum x1, blocking collectives, body(): lax.psum(local_bias.astype(jnp.bfloat16), 'image').astype(jnp.float32)  5.67 us
  transfers between devices with their start and end apart: 9, of which 1 were waited for; matrix products, arithmetic and copies ran while one was open for 14% of the time, Pallas kernels for 0%

profile of v1, /device:TPU:0, one launch (start us, length us, event | category | flops | bytes accessed | tf_op | source)
XLA Modules:
  0.0 138.1 jit_solution(15355980808841798515)
XLA Ops:
  7.2 1.0 convert_reduce_fusion
  8.6 13.5 %all-reduce.7 = (f32[1,32]{1,0:T(1,128)S(1)}, f32[1,32]{1,0:T(1,128)S(1)}) all-reduce(f32[1,32]{1,0:T(1,128)S(1)} %bitcast.142, f32[1,32]{1,0:T(1,128)S(1)} %bitcast.144), channel_id=1, replica_groups=mesh['groups'=2,'tile'=4,'image'=4] {'tile'}, use_global_device_ids=true, to_apply=%region_5.6 | all-reduce | flops 64 | bytes 512 | tf_op jit(solution)/shard_map/psum | solution.py:66
  22.5 1.0 fusion.15
  24.1 1.3 collective-permute-start.1
  25.4 4.5 %collective-permute-start = (bf16[1,1,64,256]{3,2,1,0:T(8,128)(2,1)}, bf16[1,1,64,256]{3,2,1,0:T(8,128)(2,1)S(1)}, u32[]{:S(2)}, u32[]{:S(2)}) collective-permute-start(bf16[1,1,64,256]{3,2,1,0:T(8,128)(2,1)} %get-tuple-element.63), channel_id=1, source_target_pairs={{0,4},{4,8},{8,12},{1,5},{5,9},{9,13},{2,6},{6,10},{10,14},{3,7},{... | collective-permute-start | bytes 98312 | tf_op jit(solution)/shard_map/ppermute | solution.py:16
  30.0 1.4 %fusion.53 = (bf16[1,1,64,256]{3,2,1,0:T(8,128)(2,1)}, bf16[1,1,64,256]{3,2,1,0:T(8,128)(2,1)}) fusion(bf16[1,4,64,256]{3,2,1,0:T(8,128)(2,1)} %param.14), kind=kLoop, calls=%fused_computation.108 | loop fusion | bytes 131072 | tf_op jit(solution)/shard_map/slice | solution.py:19
  31.4 1.9 %collective-permute-start.4 = (bf16[1,1,64,256]{3,2,1,0:T(8,128)(2,1)}, bf16[1,1,64,256]{3,2,1,0:T(8,128)(2,1)S(1)}, u32[]{:S(2)}, u32[]{:S(2)}) collective-permute-start(bf16[1,1,64,256]{3,2,1,0:T(8,128)(2,1)} %get-tuple-element.60), channel_id=1, source_target_pairs={{0,4},{4,8},{8,12},{1,5},{5,9},{9,13},{2,6},{6,10},{10,14},{3,7},{... | collective-permute-start | bytes 98312 | tf_op jit(solution)/shard_map/ppermute | solution.py:16
  33.3 1.4 %collective-permute-start.5 = (bf16[1,1,64,256]{3,2,1,0:T(8,128)(2,1)}, bf16[1,1,64,256]{3,2,1,0:T(8,128)(2,1)S(1)}, u32[]{:S(2)}, u32[]{:S(2)}) collective-permute-start(bf16[1,1,64,256]{3,2,1,0:T(8,128)(2,1)} %get-tuple-element.59), channel_id=1, source_target_pairs={{4,0},{8,4},{12,8},{5,1},{9,5},{13,9},{6,2},{10,6},{14,10},{7,3},{... | collective-permute-start | bytes 98312 | tf_op jit(solution)/shard_map/ppermute | solution.py:19
  34.7 2.4 %copy.19 = bf16[3,3,256,256]{2,3,1,0:T(8,128)(2,1)} copy(bf16[3,3,256,256]{3,2,1,0:T(8,128)(2,1)} %param.20) | data formatting | bytes 2359296 | tf_op args[7]
  38.7 1.0 fusion.44
  39.7 1.6 %copy.20 = bf16[3,3,256,256]{2,3,1,0:T(8,128)(2,1)} copy(bf16[3,3,256,256]{3,2,1,0:T(8,128)(2,1)S(1)} %copy-done.2) | data formatting | bytes 2359296 | tf_op args[6]
  42.9 1.0 fusion.31
  44.0 1.2 convolution_bitcast_fusion
  45.2 11.9 %all-gather.1 = f32[4,1,512]{2,1,0:T(1,128)S(1)} all-gather(f32[1,1,512]{2,1,0:T(1,128)S(1)} %convolution_bitcast_fusion), channel_id=2, replica_groups=mesh['groups'=2,'tile'=4,'image'=4] {'tile'}, dimensions={0}, use_global_device_ids=true | all-gather | bytes 10240 | tf_op jit(solution)/shard_map/all_gather | solution.py:130
  62.5 10.1 %all-reduce.6 = (f32[1,32]{1,0:T(1,128)S(1)}, f32[1,32]{1,0:T(1,128)S(1)}) all-reduce(f32[1,32]{1,0:T(1,128)S(1)} %bitcast.141, f32[1,32]{1,0:T(1,128)S(1)} %bitcast.145), channel_id=1, replica_groups=mesh['groups'=2,'tile'=4,'image'=4] {'tile'}, use_global_device_ids=true, to_apply=%region_11.12 | all-reduce | flops 64 | bytes 512 | tf_op jit(solution)/shard_map/psum | solution.py:66
  75.4 8.7 %all-reduce.5 = (f32[1,256]{1,0:T(1,128)S(1)}, f32[1,256]{1,0:T(1,128)S(1)}) all-reduce(f32[1,256]{1,0:T(1,128)S(1)} %bitcast.138, f32[1,256]{1,0:T(1,128)S(1)} %bitcast.139), channel_id=1, replica_groups=mesh['groups'=2,'tile'=4,'image'=4] {'tile'}, use_global_device_ids=true, to_apply=%region_14.15 | all-reduce | flops 512 | bytes 4096 | tf_op jit(solution)/shard_map/psum | solution.py:153
  85.1 1.3 collective-permute-start.3
  86.4 4.5 %collective-permute-start.2 = (bf16[1,1,64,256]{3,2,1,0:T(8,128)(2,1)S(1)}, bf16[1,1,64,256]{3,2,1,0:T(8,128)(2,1)S(1)}, u32[]{:S(2)}, u32[]{:S(2)}) collective-permute-start(bf16[1,1,64,256]{3,2,1,0:T(8,128)(2,1)S(1)} %get-tuple-element.61), channel_id=1, source_target_pairs={{0,4},{4,8},{8,12},{1,5},{5,9},{9,13},{2,6},{6,10},{10,14},{3,7},{... | collective-permute-start | bytes 98312 | tf_op jit(solution)/shard_map/ppermute | solution.py:16
  91.8 1.3 collective-permute-start.7
  93.1 4.5 %collective-permute-start.6 = (bf16[1,1,64,256]{3,2,1,0:T(8,128)(2,1)S(1)}, bf16[1,1,64,256]{3,2,1,0:T(8,128)(2,1)S(1)}, u32[]{:S(2)}, u32[]{:S(2)}) collective-permute-start(bf16[1,1,64,256]{3,2,1,0:T(8,128)(2,1)S(1)} %get-tuple-element.57), channel_id=1, source_target_pairs={{0,4},{4,8},{8,12},{1,5},{5,9},{9,13},{2,6},{6,10},{10,14},{3,7},{... | collective-permute-start | bytes 98312 | tf_op jit(solution)/shard_map/ppermute | solution.py:16
  97.7 5.7 %psum.79 = bf16[512]{0:T(512)(128)(2,1)S(1)} all-reduce(bf16[512]{0:T(512)(128)(2,1)S(1)} %convert_element_type.135), channel_id=1, replica_groups=mesh['groups'=2,'tile'=4,'image'=4] {'image'}, use_global_device_ids=true, to_apply=%region_26.27 | all-reduce | flops 512 | bytes 2048 | tf_op jit(solution)/shard_map/psum | solution.py:176
  107.1 10.1 %all-reduce.4 = (f32[1,32]{1,0:T(1,128)S(1)}, f32[1,32]{1,0:T(1,128)S(1)}) all-reduce(f32[1,32]{1,0:T(1,128)S(1)} %bitcast.140, f32[1,32]{1,0:T(1,128)S(1)} %bitcast.143), channel_id=1, replica_groups=mesh['groups'=2,'tile'=4,'image'=4] {'tile'}, use_global_device_ids=true, to_apply=%region_24.25 | all-reduce | flops 64 | bytes 512 | tf_op jit(solution)/shard_map/psum | solution.py:88
  119.7 9.7 %all-reduce.10.cloned.1.call-done = bf16[256,512]{1,0:T(8,128)(2,1)} async-done(((bf16[256,512]{1,0:T(8,128)(2,1)}), bf16[256,512]{1,0:T(8,128)(2,1)}) %all-reduce.10.cloned.1.call-update) | async-done | bytes 262160 | tf_op jit(solution)/shard_map/psum | solution.py:175
  129.4 1.8 %convert_element_type.134 = f32[256,512]{1,0:T(8,128)} convert(bf16[256,512]{1,0:T(8,128)(2,1)} %all-reduce.10.cloned.1.call-done) | non-fusion elementwise | flops 131072 | bytes 786432 | tf_op jit(solution)/shard_map/convert_element_type | solution.py:175
  (140 shorter events, 19.2 us)
Async XLA Ops:
  7.2 35.5 %copy-start = (bf16[1000,256]{1,0:T(8,128)(2,1)S(1)}, bf16[1000,256]{1,0:T(8,128)(2,1)}, u32[]{:S(2)}) copy-start(bf16[1000,256]{1,0:T(8,128)(2,1)} %param.23) | copy-start | bytes 1536004
  7.2 122.3 %all-reduce.10.cloned.1.call-start = ((), (), s32[]{:S(2)}) async-start(), calls=%async_computation | async-start | bytes 524288 | tf_op jit(solution)/shard_map/psum | solution.py:175
  24.1 35.4 %collective-permute-start.1 = (bf16[1,1,64,256]{3,2,1,0:T(8,128)(2,1)}, bf16[1,1,64,256]{3,2,1,0:T(8,128)(2,1)S(1)}, u32[]{:S(2)}, u32[]{:S(2)}) collective-permute-start(bf16[1,1,64,256]{3,2,1,0:T(8,128)(2,1)} %get-tuple-element.64), channel_id=1, source_target_pairs={{4,0},{8,4},{12,8},{5,1},{9,5},{13,9},{6,2},{10,6},{14,10},{7,3},{... | collective-permute-start | bytes 98312 | tf_op jit(solution)/shard_map/ppermute | solution.py:19
  25.4 34.1 %collective-permute-start = (bf16[1,1,64,256]{3,2,1,0:T(8,128)(2,1)}, bf16[1,1,64,256]{3,2,1,0:T(8,128)(2,1)S(1)}, u32[]{:S(2)}, u32[]{:S(2)}) collective-permute-start(bf16[1,1,64,256]{3,2,1,0:T(8,128)(2,1)} %get-tuple-element.63), channel_id=1, source_target_pairs={{0,4},{4,8},{8,12},{1,5},{5,9},{9,13},{2,6},{6,10},{10,14},{3,7},{... | collective-permute-start | bytes 98312 | tf_op jit(solution)/shard_map/ppermute | solution.py:16
  31.4 41.2 %collective-permute-start.4 = (bf16[1,1,64,256]{3,2,1,0:T(8,128)(2,1)}, bf16[1,1,64,256]{3,2,1,0:T(8,128)(2,1)S(1)}, u32[]{:S(2)}, u32[]{:S(2)}) collective-permute-start(bf16[1,1,64,256]{3,2,1,0:T(8,128)(2,1)} %get-tuple-element.60), channel_id=1, source_target_pairs={{0,4},{4,8},{8,12},{1,5},{5,9},{9,13},{2,6},{6,10},{10,14},{3,7},{... | collective-permute-start | bytes 98312 | tf_op jit(solution)/shard_map/ppermute | solution.py:16
  33.3 3.8 %copy-start.1 = (bf16[3,3,256,256]{3,2,1,0:T(8,128)(2,1)S(1)}, bf16[3,3,256,256]{3,2,1,0:T(8,128)(2,1)}, u32[]{:S(2)}) copy-start(bf16[3,3,256,256]{3,2,1,0:T(8,128)(2,1)} %param.20) | copy-start | bytes 3538948
  33.3 39.7 %collective-permute-start.5 = (bf16[1,1,64,256]{3,2,1,0:T(8,128)(2,1)}, bf16[1,1,64,256]{3,2,1,0:T(8,128)(2,1)S(1)}, u32[]{:S(2)}, u32[]{:S(2)}) collective-permute-start(bf16[1,1,64,256]{3,2,1,0:T(8,128)(2,1)} %get-tuple-element.59), channel_id=1, source_target_pairs={{4,0},{8,4},{12,8},{5,1},{9,5},{13,9},{6,2},{10,6},{14,10},{7,3},{... | collective-permute-start | bytes 98312 | tf_op jit(solution)/shard_map/ppermute | solution.py:19
  37.1 1.6 %copy-start.2 = (bf16[3,3,256,256]{3,2,1,0:T(8,128)(2,1)S(1)}, bf16[3,3,256,256]{3,2,1,0:T(8,128)(2,1)}, u32[]{:S(2)}) copy-start(bf16[3,3,256,256]{3,2,1,0:T(8,128)(2,1)} %param.19) | copy-start | bytes 3538948
  39.7 4.2 %copy-start.18 = (f32[256]{0:T(256)S(1)}, f32[256]{0:T(256)}, u32[]{:S(2)}) copy-start(f32[256]{0:T(256)} %param.22) | copy-start | bytes 3076
  39.7 17.4 %copy-start.3 = (bf16[3,3,256,256]{2,3,1,0:T(8,128)(2,1)S(1)}, bf16[3,3,256,256]{2,3,1,0:T(8,128)(2,1)}, u32[]{:S(2)}) copy-start(bf16[3,3,256,256]{2,3,1,0:T(8,128)(2,1)} %copy.19) | copy-start | bytes 3538948
  57.2 1.6 %copy-start.4 = (bf16[3,3,256,256]{2,3,1,0:T(8,128)(2,1)S(1)}, bf16[3,3,256,256]{2,3,1,0:T(8,128)(2,1)}, u32[]{:S(2)}) copy-start(bf16[3,3,256,256]{2,3,1,0:T(8,128)(2,1)} %copy.20) | copy-start | bytes 3538948
  59.8 1.0 copy-start.12
  59.8 1.3 copy-start.10
  60.8 1.0 copy-start.9
  61.0 11.6 %copy-start.14 = (bf16[1,4,64,256]{3,2,1,0:T(8,128)(2,1)S(1)}, bf16[1,4,64,256]{3,2,1,0:T(8,128)(2,1)}, u32[]{:S(2)}) copy-start(bf16[1,4,64,256]{3,2,1,0:T(8,128)(2,1)} %param.14) | copy-start | bytes 393220
  73.1 1.0 copy-start.8
  74.1 1.0 copy-start.13
  85.1 18.8 %collective-permute-start.3 = (bf16[1,1,64,256]{3,2,1,0:T(8,128)(2,1)S(1)}, bf16[1,1,64,256]{3,2,1,0:T(8,128)(2,1)S(1)}, u32[]{:S(2)}, u32[]{:S(2)}) collective-permute-start(bf16[1,1,64,256]{3,2,1,0:T(8,128)(2,1)S(1)} %get-tuple-element.62), channel_id=1, source_target_pairs={{4,0},{8,4},{12,8},{5,1},{9,5},{13,9},{6,2},{10,6},{14,10},{7,3},{... | collective-permute-start | bytes 98312 | tf_op jit(solution)/shard_map/ppermute | solution.py:19
  86.4 17.5 %collective-permute-start.2 = (bf16[1,1,64,256]{3,2,1,0:T(8,128)(2,1)S(1)}, bf16[1,1,64,256]{3,2,1,0:T(8,128)(2,1)S(1)}, u32[]{:S(2)}, u32[]{:S(2)}) collective-permute-start(bf16[1,1,64,256]{3,2,1,0:T(8,128)(2,1)S(1)} %get-tuple-element.61), channel_id=1, source_target_pairs={{0,4},{4,8},{8,12},{1,5},{5,9},{9,13},{2,6},{6,10},{10,14},{3,7},{... | collective-permute-start | bytes 98312 | tf_op jit(solution)/shard_map/ppermute | solution.py:16
  91.8 13.2 %collective-permute-start.7 = (bf16[1,1,64,256]{3,2,1,0:T(8,128)(2,1)S(1)}, bf16[1,1,64,256]{3,2,1,0:T(8,128)(2,1)S(1)}, u32[]{:S(2)}, u32[]{:S(2)}) collective-permute-start(bf16[1,1,64,256]{3,2,1,0:T(8,128)(2,1)S(1)} %get-tuple-element.58), channel_id=1, source_target_pairs={{4,0},{8,4},{12,8},{5,1},{9,5},{13,9},{6,2},{10,6},{14,10},{7,3},{... | collective-permute-start | bytes 98312 | tf_op jit(solution)/shard_map/ppermute | solution.py:19
  93.1 11.9 %collective-permute-start.6 = (bf16[1,1,64,256]{3,2,1,0:T(8,128)(2,1)S(1)}, bf16[1,1,64,256]{3,2,1,0:T(8,128)(2,1)S(1)}, u32[]{:S(2)}, u32[]{:S(2)}) collective-permute-start(bf16[1,1,64,256]{3,2,1,0:T(8,128)(2,1)S(1)} %get-tuple-element.57), channel_id=1, source_target_pairs={{0,4},{4,8},{8,12},{1,5},{5,9},{9,13},{2,6},{6,10},{10,14},{3,7},{... | collective-permute-start | bytes 98312 | tf_op jit(solution)/shard_map/ppermute | solution.py:16
  105.9 11.6 %copy-start.7 = (bf16[1,3,256,256]{3,2,1,0:T(8,128)(2,1)S(1)}, bf16[1,3,256,256]{3,2,1,0:T(8,128)(2,1)}, u32[]{:S(2)}) copy-start(bf16[1,3,256,256]{3,2,1,0:T(8,128)(2,1)} %get-tuple-element.31) | copy-start | bytes 1179652
  105.9 11.6 %copy-start.11 = (bf16[1,4,64,768]{3,2,1,0:T(8,128)(2,1)S(1)}, bf16[1,4,64,768]{3,2,1,0:T(8,128)(2,1)}, u32[]{:S(2)}) copy-start(bf16[1,4,64,768]{3,2,1,0:T(8,128)(2,1)} %get-tuple-element.43) | copy-start | bytes 1179652
  106.5 11.3 %copy-start.6 = (bf16[1,3,256,256]{3,2,1,0:T(8,128)(2,1)S(1)}, bf16[1,3,256,256]{3,2,1,0:T(8,128)(2,1)}, u32[]{:S(2)}) copy-start(bf16[1,3,256,256]{3,2,1,0:T(8,128)(2,1)} %get-tuple-element.30) | copy-start | bytes 1179652
  (4 other events, 3.4 us)
Sparse Core Ops, SparseCore 0:
  97.8 31.5 all-reduce.9
